TPU v7x, 512 devices: a whole 4x4x16 slice. The times are simulated.
512 devices in a mesh: test: 8 (over z_lo, core), bx: 4 (over y), by: 16 (over z_hi, x).
Axes of the slice: x: 4, y: 4, z: 16 (z_hi: 4, z_lo: 4; z = z_hi * 4 + z_lo), core: 2. Of those that a mesh axis runs over, the one named last changes fastest.
Arguments:
- log_conductivity: float32 [32, 128, 256], P('bx', 'by'), may hold values from -3 to 3
- storage: float32 [32, 128, 256], P('bx', 'by'), may hold values from 0.5 to 2
- recharge: float32 [32, 128, 256], P('bx', 'by'), may hold values from -6 to 6
- pump_rate: float32 [32], P('test'), may hold values from 4 to 16
- pump_well: int32 [32], P('test'), may hold values from 0 to 2047
- observed: float32 [32, 2048], P('test'), may hold values from -9 to 9
- owner: int32 [2048], replicated, may hold values from 0 to 63, as said below
- screen_column: int32 [2048], replicated, may hold values from 0 to 63
- screen_top: int32 [2048], replicated, may hold values from 0 to 248
Outputs:
- gradient: float32 [32, 128, 256], P('bx', 'by', 'test')
Inputs may be any that keep to these rules, and one draw needn't show every extreme that they name: `owner`: each brick owns exactly 32 wells.
All inputs are finite; a program needn't handle non-finite values.
Results may differ from a plain program's by a relative error of at most 0.0001.
Values sent between devices are 32-bit elements; how exact they have to be, the bound alone decides.
A program may use at most 64 MiB of HBM per device.

v0:
```python
import jax
import jax.numpy as jnp
from jax import lax
from jax.sharding import PartitionSpec as P

SWEEPS = 3
SCREEN = 8
epsilon = 1e-06


def with_halo(block, sides, width):
    for axis, dim in sides:
        count = lax.axis_size(axis)
        forward = [(i, i + 1) for i in range(count - 1)]
        backward = [(target, source) for source, target in forward]
        low = lax.ppermute(
            lax.slice_in_dim(block, block.shape[dim] - width, None, axis=dim), axis, forward
        )
        high = lax.ppermute(lax.slice_in_dim(block, 0, width, axis=dim), axis, backward)
        block = jnp.concatenate([low, block, high], axis=dim)
    return block


def pad_depth(values):
    return jnp.pad(values, [(0, 0)] * (values.ndim - 1) + [(1, 1)])


def neighbours(padded, centre):
    z_padded = pad_depth(centre)
    return [
        padded[..., 2:, 1:-1, :],
        padded[..., :-2, 1:-1, :],
        padded[..., 1:-1, 2:, :],
        padded[..., 1:-1, :-2, :],
        z_padded[..., 2:],
        z_padded[..., :-2],
    ]


def weighted(conductance, others):
    accumulated = conductance[0] * others[0]
    for position in range(1, 6):
        accumulated = accumulated + conductance[position] * others[position]
    return accumulated


def sensitivity(conductance, heads_field, heads_padded, adjoint_field, adjoint_padded):
    near_heads = neighbours(heads_padded, heads_field)
    near_adjoint = neighbours(adjoint_padded, adjoint_field)
    accumulated = jnp.zeros_like(heads_field)
    for position in range(6):
        accumulated = accumulated + conductance[position] * (heads_field - near_heads[position]) * (
            adjoint_field - near_adjoint[position]
        )
    return -0.5 * accumulated


def relax_field(source, conductance, diagonal):
    iterate = source / diagonal
    for sweep_index in range(SWEEPS - 1):
        padded = with_halo(iterate, (("bx", 1), ("by", 2)), 1)
        iterate = (source + weighted(conductance, neighbours(padded, iterate))) / diagonal
    return iterate


def per_sweep_terms(
    log_conductivity,
    storage,
    recharge,
    pump_rate,
    pump_well,
    observed,
    owner,
    screen_column,
    screen_top,
):
    size_x, size_y, size_z = log_conductivity.shape
    tests_here = pump_rate.shape[0]
    cell_count = size_x * size_y * size_z
    padded_log = with_halo(log_conductivity, (("bx", 0), ("by", 1)), 1)
    conductance = [
        jnp.exp(0.5 * (log_conductivity + other))
        for other in neighbours(padded_log, log_conductivity)
    ]
    diagonal = storage + weighted(conductance, [1.0] * 6)
    brick_index = lax.axis_index("bx") * lax.axis_size("by") + lax.axis_index("by")
    offsets = jnp.arange(SCREEN, dtype=jnp.int32)
    screen_cells = (screen_column * size_z + screen_top)[:, None] + offsets[None, :]
    owned_here = owner == brick_index
    pump_cells = screen_cells[pump_well]
    pump_value = jnp.where(owner[pump_well] == brick_index, -pump_rate, 0.0)
    test_rows = jnp.arange(tests_here, dtype=jnp.int32)[:, None]
    flat_source = jnp.broadcast_to(recharge.reshape(1, cell_count), (tests_here, cell_count))
    flat_source = flat_source.at[test_rows, pump_cells].add(
        jnp.broadcast_to(pump_value[:, None], pump_cells.shape)
    )
    source = flat_source.reshape(tests_here, size_x, size_y, size_z)
    heads_field = relax_field(source, conductance, diagonal)
    well_heads = jnp.mean(heads_field.reshape(tests_here, cell_count)[:, screen_cells], axis=2)
    residual = jnp.where(owned_here[None, :], well_heads - observed, 0.0)
    well_count = residual.shape[1]
    misfit = lax.psum(jnp.sum(residual * residual, axis=1), ("bx", "by")) / well_count + epsilon
    weights = residual / misfit[:, None]
    values = jnp.broadcast_to(weights[:, :, None], (tests_here, well_count, SCREEN)).reshape(
        tests_here, -1
    )
    adjoint_source = (
        jnp.zeros((tests_here, cell_count), jnp.float32).at[:, screen_cells.reshape(-1)].add(values)
    )
    adjoint_field = relax_field(
        adjoint_source.reshape(tests_here, size_x, size_y, size_z), conductance, diagonal
    )
    stacked = with_halo(
        jnp.concatenate([heads_field, adjoint_field], axis=0), (("bx", 1), ("by", 2)), 1
    )
    test_terms = sensitivity(
        conductance, heads_field, stacked[:tests_here], adjoint_field, stacked[tests_here:]
    )
    return (test_terms, misfit)


def local(
    log_conductivity,
    storage,
    recharge,
    pump_rate,
    pump_well,
    observed,
    owner,
    screen_column,
    screen_top,
):
    size_z = log_conductivity.shape[2]
    tests_here = pump_rate.shape[0]
    test_terms, misfit = per_sweep_terms(
        log_conductivity,
        storage,
        recharge,
        pump_rate,
        pump_well,
        observed,
        owner,
        screen_column,
        screen_top,
    )
    local_sum = jnp.sum(test_terms, axis=0)
    all_tests = tests_here * lax.axis_size("test")
    grand_total = lax.psum(local_sum, "test")
    slab_depth = size_z // lax.axis_size("test")
    gradient = lax.dynamic_slice_in_dim(
        grand_total, lax.axis_index("test") * slab_depth, slab_depth, 2
    )
    return gradient / all_tests


def solution(mesh):
    placed = (
        P("bx", "by", None),
        P("bx", "by", None),
        P("bx", "by", None),
        P("test"),
        P("test"),
        P("test", None),
        P(),
        P(),
        P(),
    )
    return jax.shard_map(
        local, mesh=mesh, in_specs=placed, out_specs=P("bx", "by", "test"), check_vma=False
    )
```

profile of v0, /device:TPU:2, one launch (start us, length us, event | category | flops | bytes accessed | tf_op | source)
XLA Modules:
  0.0 626.8 jit_solution(6473687219000279522)
XLA Ops:
  7.3 3.5 collective-permute-start.1
  10.7 1.3 collective-permute-start
  14.3 1.3 gather_fusion.1
  16.6 5.6 collective-permute-start.2
  22.2 1.9 collective-permute-start.3
  25.0 0.9 copy.25
  26.0 2.1 scatter_fusion
  28.1 1.2 add_add_fusion
  29.5 1.3 collective-permute-start.4
  30.8 5.2 collective-permute-start.5
  36.0 1.6 collective-permute-done.5
  37.6 3.9 collective-permute-start.6
  41.5 1.9 collective-permute-start.7
  44.3 3.1 collective-permute-done.7
  48.0 1.1 fusion.9
  49.1 1.3 collective-permute-start.8
  50.4 4.9 collective-permute-start.9
  55.3 1.5 collective-permute-done.9
  56.9 1.9 collective-permute-start.10
  58.8 4.6 collective-permute-start.11
  64.0 1.1 copy.21
  65.4 4.7 copy.20
  70.1 58.2 %gather_fusion.2 = f32[16384,4]{1,0:T(8,128)} fusion(f32[4,16384]{0,1:T(8,128)} %bitcast.34, s32[16384]{0:T(1024)S(1)} %broadcast_clamp_fusion), kind=kCustom, calls=%fused_computation.2 | custom fusion | bytes 589824 | tf_op jit(solution)/shard_map/gather | solution.py:99
  128.3 13.0 %bitcast_reduce_fusion = f32[2048,4]{1,0:T(8,128)S(1)} fusion(f32[16384,4]{1,0:T(8,128)} %gather_fusion.2), kind=kLoop, calls=%fused_computation.7 | loop fusion | flops 57344 | bytes 294912 | tf_op jit(solution)/shard_map/reduce_sum | solution.py:99
  142.5 236.4 %psum.14 = f32[4]{0:T(128)S(1)} all-reduce(f32[4]{0:T(128)S(1)} %multiply_reduce_fusion), channel_id=1, replica_groups=mesh['test'=8,'bx'=4,'by'=16] {'bx','by'}, use_global_device_ids=true, to_apply=%region_3.4 | all-reduce | flops 4 | bytes 32 | tf_op jit(solution)/shard_map/psum | solution.py:102
  379.4 91.6 %scatter_custom_fusion.1 = f32[4,16384]{0,1:T(8,128)} fusion(s32[16384]{0:T(1024)} %bitcast.41, f32[4,2048]{0,1:T(8,128)S(1)} %broadcast_divide_fusion, f32[]{:T(128)} %constant.27.clone.1), kind=kCustom, calls=%fused_computation.5 | custom fusion | flops 65536 | bytes 295424 | tf_op jit(solution)/shard_map/scatter-add | solution.py:108
  471.0 5.2 copy.24
  476.3 1.3 collective-permute-start.12
  477.6 4.5 collective-permute-start.13
  482.1 1.6 collective-permute-done.13
  483.8 4.0 collective-permute-start.14
  487.8 1.9 collective-permute-start.15
  489.7 4.0 collective-permute-done.15
  493.9 1.3 collective-permute-start.16
  495.2 4.9 collective-permute-start.17
  500.1 1.6 collective-permute-done.17
  501.7 1.9 collective-permute-start.18
  503.7 3.9 collective-permute-start.19
  507.6 1.9 collective-permute-done.19
  509.8 1.3 collective-permute-start.20
  511.1 4.9 collective-permute-start.21
  516.3 1.6 collective-permute-done.21
  518.0 1.9 collective-permute-start.22
  519.9 3.9 collective-permute-start.23
  524.3 1.9 collective-permute-done.23
  526.2 1.1 fusion.35
  527.4 91.2 %all-reduce.9.cloned.1.call-done = f32[8,8,256]{2,1,0:T(8,128)} async-done(((f32[8,8,256]{2,1,0:T(8,128)}), f32[8,8,256]{2,1,0:T(8,128)}) %all-reduce.9.cloned.1.call-update) | async-done | bytes 65552 | tf_op jit(solution)/shard_map/psum | solution.py:148
  618.5 1.4 dynamic-slice_multiply_fusion
  (83 shorter events, 10.5 us)
Async XLA Ops:
  6.5 56.9 %copy-start = (s32[2048]{0:T(1024)S(1)}, s32[2048]{0:T(1024)}, u32[]{:S(2)}) copy-start(s32[2048]{0:T(1024)} %param.15) | copy-start | bytes 24580
  6.5 612.0 %all-reduce.9.cloned.1.call-start = ((), (), s32[]{:S(2)}) async-start(), calls=%async_computation | async-start | bytes 131072 | tf_op jit(solution)/shard_map/psum | solution.py:148
  7.3 8.4 %collective-permute-start.1 = (f32[1,8,256]{2,1,0:T(8,128)S(1)}, f32[1,8,256]{2,1,0:T(8,128)S(1)}, u32[]{:S(2)}, u32[]{:S(2)}) collective-permute-start(f32[1,8,256]{2,1,0:T(8,128)S(1)} %get-tuple-element.35), channel_id=1, source_target_pairs={{0,16},{16,32},{32,48},{1,17},{17,33},{33,49},{2,18},{18,34},{34,5... | collective-permute-start | bytes 24584 | tf_op jit(solution)/shard_map/ppermute | solution.py:16
  10.7 5.8 collective-permute-start
  16.6 11.5 %collective-permute-start.2 = (f32[10,1,256]{2,1,0:T(1,128)S(1)}, f32[10,1,256]{2,1,0:T(1,128)S(1)}, u32[]{:S(2)}, u32[]{:S(2)}) collective-permute-start(f32[10,1,256]{2,1,0:T(1,128)S(1)} %get-tuple-element.33), channel_id=1, source_target_pairs={{1,0},{2,1},{3,2},{4,3},{5,4},{6,5},{7,6},{8,7},{9,8},{10,9},{11,1... | collective-permute-start | bytes 30728 | tf_op jit(solution)/shard_map/ppermute | solution.py:19
  22.2 5.9 collective-permute-start.3
  29.3 40.8 %copy-start.1 = (f32[8,8,256]{2,1,0:T(8,128)}, f32[8,8,256]{2,1,0:T(8,128)S(1)}, u32[]{:S(2)}) copy-start(f32[8,8,256]{2,1,0:T(8,128)S(1)} %get-tuple-element.7) | copy-start | bytes 196612
  29.3 40.8 %copy-start.3 = (f32[8,8,256]{2,1,0:T(8,128)}, f32[8,8,256]{2,1,0:T(8,128)S(1)}, u32[]{:S(2)}) copy-start(f32[8,8,256]{2,1,0:T(8,128)S(1)} %get-tuple-element.8) | copy-start | bytes 196612
  29.4 40.8 %copy-start.5 = (f32[8,8,256]{2,1,0:T(8,128)}, f32[8,8,256]{2,1,0:T(8,128)S(1)}, u32[]{:S(2)}) copy-start(f32[8,8,256]{2,1,0:T(8,128)S(1)} %get-tuple-element.9) | copy-start | bytes 196612
  29.4 40.8 %copy-start.7 = (f32[8,8,256]{2,1,0:T(8,128)}, f32[8,8,256]{2,1,0:T(8,128)S(1)}, u32[]{:S(2)}) copy-start(f32[8,8,256]{2,1,0:T(8,128)S(1)} %get-tuple-element.10) | copy-start | bytes 196612
  29.4 40.8 %copy-start.9 = (f32[8,8,256]{2,1,0:T(8,128)}, f32[8,8,256]{2,1,0:T(8,128)S(1)}, u32[]{:S(2)}) copy-start(f32[8,8,256]{2,1,0:T(8,128)S(1)} %get-tuple-element.11) | copy-start | bytes 196612
  29.5 6.5 %collective-permute-start.4 = (f32[4,1,8,256]{3,2,1,0:T(8,128)S(1)}, f32[4,1,8,256]{3,2,1,0:T(8,128)S(1)}, u32[]{:S(2)}, u32[]{:S(2)}) collective-permute-start(f32[4,1,8,256]{3,2,1,0:T(8,128)S(1)} %get-tuple-element.31), channel_id=1, source_target_pairs={{16,0},{32,16},{48,32},{17,1},{33,17},{49,33},{18,2},{34,18},{50,3... | collective-permute-start | bytes 98312 | tf_op jit(solution)/shard_map/ppermute | solution.py:19
  30.8 6.8 %collective-permute-start.5 = (f32[4,1,8,256]{3,2,1,0:T(8,128)S(1)}, f32[4,1,8,256]{3,2,1,0:T(8,128)S(1)}, u32[]{:S(2)}, u32[]{:S(2)}) collective-permute-start(f32[4,1,8,256]{3,2,1,0:T(8,128)S(1)} %get-tuple-element.30), channel_id=1, source_target_pairs={{0,16},{16,32},{32,48},{1,17},{17,33},{33,49},{2,18},{18,34},{34,5... | collective-permute-start | bytes 98312 | tf_op jit(solution)/shard_map/ppermute | solution.py:16
  37.6 6.7 %collective-permute-start.6 = (f32[4,10,1,256]{3,2,1,0:T(1,128)S(1)}, f32[4,10,1,256]{3,2,1,0:T(1,128)S(1)}, u32[]{:S(2)}, u32[]{:S(2)}) collective-permute-start(f32[4,10,1,256]{3,2,1,0:T(1,128)S(1)} %get-tuple-element.22), channel_id=1, source_target_pairs={{1,0},{2,1},{3,2},{4,3},{5,4},{6,5},{7,6},{8,7},{9,8},{10,9},{11,1... | collective-permute-start | bytes 122888 | tf_op jit(solution)/shard_map/ppermute | solution.py:19
  41.5 5.9 collective-permute-start.7
  44.3 3.1 copy-start.11
  47.4 0.6 copy-start.12
  49.1 6.2 collective-permute-start.8
  50.4 6.4 %collective-permute-start.9 = (f32[4,1,8,256]{3,2,1,0:T(8,128)S(1)}, f32[4,1,8,256]{3,2,1,0:T(8,128)S(1)}, u32[]{:S(2)}, u32[]{:S(2)}) collective-permute-start(f32[4,1,8,256]{3,2,1,0:T(8,128)S(1)} %get-tuple-element.28), channel_id=1, source_target_pairs={{0,16},{16,32},{32,48},{1,17},{17,33},{33,49},{2,18},{18,34},{34,5... | collective-permute-start | bytes 98312 | tf_op jit(solution)/shard_map/ppermute | solution.py:16
  56.9 8.2 %collective-permute-start.10 = (f32[4,10,1,256]{3,2,1,0:T(1,128)S(1)}, f32[4,10,1,256]{3,2,1,0:T(1,128)S(1)}, u32[]{:S(2)}, u32[]{:S(2)}) collective-permute-start(f32[4,10,1,256]{3,2,1,0:T(1,128)S(1)} %get-tuple-element.20), channel_id=1, source_target_pairs={{1,0},{2,1},{3,2},{4,3},{5,4},{6,5},{7,6},{8,7},{9,8},{10,9},{11,1... | collective-permute-start | bytes 122888 | tf_op jit(solution)/shard_map/ppermute | solution.py:19
  58.8 6.3 %collective-permute-start.11 = (f32[4,10,1,256]{3,2,1,0:T(1,128)S(1)}, f32[4,10,1,256]{3,2,1,0:T(1,128)S(1)}, u32[]{:S(2)}, u32[]{:S(2)}) collective-permute-start(f32[4,10,1,256]{3,2,1,0:T(1,128)S(1)} %get-tuple-element.21), channel_id=1, source_target_pairs={{0,1},{1,2},{2,3},{3,4},{4,5},{5,6},{6,7},{7,8},{8,9},{9,10},{10,1... | collective-permute-start | bytes 122888 | tf_op jit(solution)/shard_map/ppermute | solution.py:16
  379.4 114.3 %copy-start.2 = (f32[8,8,256]{2,1,0:T(8,128)S(1)}, f32[8,8,256]{2,1,0:T(8,128)}, u32[]{:S(2)}) copy-start(f32[8,8,256]{2,1,0:T(8,128)} %copy-done.1) | copy-start | bytes 196612
  379.4 114.3 %copy-start.4 = (f32[8,8,256]{2,1,0:T(8,128)S(1)}, f32[8,8,256]{2,1,0:T(8,128)}, u32[]{:S(2)}) copy-start(f32[8,8,256]{2,1,0:T(8,128)} %copy-done.3) | copy-start | bytes 196612
  379.4 114.3 %copy-start.6 = (f32[8,8,256]{2,1,0:T(8,128)S(1)}, f32[8,8,256]{2,1,0:T(8,128)}, u32[]{:S(2)}) copy-start(f32[8,8,256]{2,1,0:T(8,128)} %copy-done.5) | copy-start | bytes 196612
  379.4 114.3 %copy-start.8 = (f32[8,8,256]{2,1,0:T(8,128)S(1)}, f32[8,8,256]{2,1,0:T(8,128)}, u32[]{:S(2)}) copy-start(f32[8,8,256]{2,1,0:T(8,128)} %copy-done.7) | copy-start | bytes 196612
  379.4 114.3 %copy-start.10 = (f32[8,8,256]{2,1,0:T(8,128)S(1)}, f32[8,8,256]{2,1,0:T(8,128)}, u32[]{:S(2)}) copy-start(f32[8,8,256]{2,1,0:T(8,128)} %copy-done.9) | copy-start | bytes 196612
  476.3 5.9 collective-permute-start.12
  477.6 6.1 collective-permute-start.13
  483.8 5.9 collective-permute-start.14
  487.8 5.9 collective-permute-start.15
  493.9 6.2 collective-permute-start.16
  495.2 6.4 %collective-permute-start.17 = (f32[4,1,8,256]{3,2,1,0:T(8,128)S(1)}, f32[4,1,8,256]{3,2,1,0:T(8,128)S(1)}, u32[]{:S(2)}, u32[]{:S(2)}) collective-permute-start(f32[4,1,8,256]{3,2,1,0:T(8,128)S(1)} %get-tuple-element.24), channel_id=1, source_target_pairs={{0,16},{16,32},{32,48},{1,17},{17,33},{33,49},{2,18},{18,34},{34,5... | collective-permute-start | bytes 98312 | tf_op jit(solution)/shard_map/ppermute | solution.py:16
  501.7 5.9 collective-permute-start.18
  503.7 5.9 collective-permute-start.19
  509.8 6.5 %collective-permute-start.20 = (f32[8,1,8,256]{3,2,1,0:T(8,128)S(1)}, f32[8,1,8,256]{3,2,1,0:T(8,128)S(1)}, u32[]{:S(2)}, u32[]{:S(2)}) collective-permute-start(f32[8,1,8,256]{3,2,1,0:T(8,128)S(1)} %get-tuple-element.15), channel_id=1, source_target_pairs={{16,0},{32,16},{48,32},{17,1},{33,17},{49,33},{18,2},{34,18},{50,3... | collective-permute-start | bytes 196616 | tf_op jit(solution)/shard_map/ppermute | solution.py:19
  511.1 6.7 %collective-permute-start.21 = (f32[8,1,8,256]{3,2,1,0:T(8,128)S(1)}, f32[8,1,8,256]{3,2,1,0:T(8,128)S(1)}, u32[]{:S(2)}, u32[]{:S(2)}) collective-permute-start(f32[8,1,8,256]{3,2,1,0:T(8,128)S(1)} %get-tuple-element.14), channel_id=1, source_target_pairs={{0,16},{16,32},{32,48},{1,17},{17,33},{33,49},{2,18},{18,34},{34,5... | collective-permute-start | bytes 196616 | tf_op jit(solution)/shard_map/ppermute | solution.py:16
  518.0 6.3 %collective-permute-start.22 = (f32[8,10,1,256]{3,2,1,0:T(1,128)S(1)}, f32[8,10,1,256]{3,2,1,0:T(1,128)S(1)}, u32[]{:S(2)}, u32[]{:S(2)}) collective-permute-start(f32[8,10,1,256]{3,2,1,0:T(1,128)S(1)} %get-tuple-element.12), channel_id=1, source_target_pairs={{1,0},{2,1},{3,2},{4,3},{5,4},{6,5},{7,6},{8,7},{9,8},{10,9},{11,1... | collective-permute-start | bytes 245768 | tf_op jit(solution)/shard_map/ppermute | solution.py:19
  519.9 6.3 %collective-permute-start.23 = (f32[8,10,1,256]{3,2,1,0:T(1,128)S(1)}, f32[8,10,1,256]{3,2,1,0:T(1,128)S(1)}, u32[]{:S(2)}, u32[]{:S(2)}) collective-permute-start(f32[8,10,1,256]{3,2,1,0:T(1,128)S(1)} %get-tuple-element.13), channel_id=1, source_target_pairs={{0,1},{1,2},{2,3},{3,4},{4,5},{5,6},{6,7},{7,8},{8,9},{9,10},{10,1... | collective-permute-start | bytes 245768 | tf_op jit(solution)/shard_map/ppermute | solution.py:16
Sparse Core Ops, SparseCore 0:
  527.5 90.9 all-reduce.8
where the time goes:
time: 628 us; the launch traced here: 627 us
  blocking collectives  236 us (38%)
  other arithmetic  117 us (19%)
  waiting for transfers between devices  111 us (18%)
  local copies, waits for them, and re-layouts  75.6 us (12%)
  starting transfers between devices  73 us (12%)
  between operations  14 us (2%)
    psum x1, blocking collectives, per_sweep_terms(): lax.psum(jnp.sum(residual * residual, axis=1), ('bx', 'by')) / well_count  236 us
    scatter-add x1, other arithmetic, per_sweep_terms(): jnp.zeros((tests_here, cell_count), jnp.float32)  91.6 us
    psum x1, waiting for transfers between devices, local(): grand_total = lax.psum(local_sum, 'test')  91.2 us
    gather x1, local copies, waits for them, and re-layouts, per_sweep_terms(): heads_field.reshape(tests_here, cell_count)[:, screen_cells]  58.2 us
    ppermute x12, starting transfers between devices, with_halo(): lax.ppermute(lax.slice_in_dim(block, block.shape[dim] - width, None, axis...  45.9 us
    ppermute x12, starting transfers between devices, with_halo(): lax.ppermute(lax.slice_in_dim(block, 0, width, axis=dim), axis, backward)  27.1 us
    ppermute x12, waiting for transfers between devices, with_halo(): lax.ppermute(lax.slice_in_dim(block, block.shape[dim] - width, None, axis...  18.8 us
    reduce_sum x1, other arithmetic, per_sweep_terms(): jnp.mean(heads_field.reshape(tests_here, cell_count)[:, screen_cells], ax...  13 us
  transfers between devices with their start and end apart: 25, of which 12 were waited for; matrix products, arithmetic and copies ran while one was open for 2% of the time, Pallas kernels for 0%

commit v1 on v0

--- a/solution.py
+++ b/solution.py
@@ -99,7 +99,9 @@
     well_heads = jnp.mean(heads_field.reshape(tests_here, cell_count)[:, screen_cells], axis=2)
     residual = jnp.where(owned_here[None, :], well_heads - observed, 0.0)
     well_count = residual.shape[1]
-    misfit = lax.psum(jnp.sum(residual * residual, axis=1), ("bx", "by")) / well_count + epsilon
+    misfit = (
+        lax.psum(lax.psum(jnp.sum(residual * residual, axis=1), "by"), "bx") / well_count + epsilon
+    )
     weights = residual / misfit[:, None]
     values = jnp.broadcast_to(weights[:, :, None], (tests_here, well_count, SCREEN)).reshape(
         tests_here, -1

time: 628 us -> 483 us (0.77)
  blocking collectives: 236 us -> 78.2 us
  waiting for transfers between devices: 111 us -> 123 us
    psum x1 -> x2, blocking collectives: 236 us -> 78.2 us  [the longest x1 65.4 us: per_sweep_terms(): lax.psum(jnp.sum(residual * residual, axis=1), 'by')]
    psum x1, waiting for transfers between devices: 91.2 us -> 103 us  [local(): grand_total = lax.psum(local_sum, 'test')]
  transfers between devices with their start and end apart: 25 -> 25, of which waited for: 12 -> 13; matrix products, arithmetic and copies ran while one was open for 2% -> 2% of each run, Pallas kernels for 0% -> 0%
where the time goes in v1:
time: 483 us; the launch traced here: 481 us
  waiting for transfers between devices  123 us (25%)
  other arithmetic  118 us (24%)
  blocking collectives  78.2 us (16%)
  local copies, waits for them, and re-layouts  74.9 us (16%)
  starting transfers between devices  72.9 us (15%)
  between operations  14 us (3%)
    psum x1, waiting for transfers between devices, local(): grand_total = lax.psum(local_sum, 'test')  103 us
    scatter-add x1, other arithmetic, per_sweep_terms(): jnp.zeros((tests_here, cell_count), jnp.float32)  91.6 us
    psum x1, blocking collectives, per_sweep_terms(): lax.psum(jnp.sum(residual * residual, axis=1), 'by')  65.4 us
    gather x1, local copies, waits for them, and re-layouts, per_sweep_terms(): heads_field.reshape(tests_here, cell_count)[:, screen_cells]  58.1 us
    ppermute x12, starting transfers between devices, with_halo(): lax.ppermute(lax.slice_in_dim(block, block.shape[dim] - width, None, axis...  46 us
    ppermute x12, starting transfers between devices, with_halo(): lax.ppermute(lax.slice_in_dim(block, 0, width, axis=dim), axis, backward)  27 us
    ppermute x12, waiting for transfers between devices, with_halo(): lax.ppermute(lax.slice_in_dim(block, block.shape[dim] - width, None, axis...  19.9 us
    reduce_sum x1, other arithmetic, per_sweep_terms(): jnp.mean(heads_field.reshape(tests_here, cell_count)[:, screen_cells], ax...  13 us
  transfers between devices with their start and end apart: 25, of which 13 were waited for; matrix products, arithmetic and copies ran while one was open for 2% of the time, Pallas kernels for 0%

profile of v1, /device:TPU:2, one launch (start us, length us, event | category | flops | bytes accessed | tf_op | source)
XLA Modules:
  0.0 481.5 jit_solution(7885473183945239675)
XLA Ops:
  7.3 3.5 collective-permute-start.1
  10.8 1.3 collective-permute-start
  14.4 1.3 gather_fusion.1
  16.6 5.6 %collective-permute-start.2 = (f32[10,1,256]{2,1,0:T(1,128)S(1)}, f32[10,1,256]{2,1,0:T(1,128)S(1)}, u32[]{:S(2)}, u32[]{:S(2)}) collective-permute-start(f32[10,1,256]{2,1,0:T(1,128)S(1)} %get-tuple-element.33), channel_id=1, source_target_pairs={{1,0},{2,1},{3,2},{4,3},{5,4},{6,5},{7,6},{8,7},{9,8},{10,9},{11,1... | collective-permute-start | bytes 30728 | tf_op jit(solution)/shard_map/ppermute | solution.py:19
  22.2 1.9 collective-permute-start.3
  26.0 2.1 scatter_fusion
  28.1 1.2 add_add_fusion
  29.5 1.3 collective-permute-start.4
  30.8 5.2 %collective-permute-start.5 = (f32[4,1,8,256]{3,2,1,0:T(8,128)S(1)}, f32[4,1,8,256]{3,2,1,0:T(8,128)S(1)}, u32[]{:S(2)}, u32[]{:S(2)}) collective-permute-start(f32[4,1,8,256]{3,2,1,0:T(8,128)S(1)} %get-tuple-element.30), channel_id=1, source_target_pairs={{0,16},{16,32},{32,48},{1,17},{17,33},{33,49},{2,18},{18,34},{34,5... | collective-permute-start | bytes 98312 | tf_op jit(solution)/shard_map/ppermute | solution.py:16
  36.0 1.6 collective-permute-done.5
  37.6 3.9 collective-permute-start.6
  41.5 1.9 collective-permute-start.7
  44.3 3.1 collective-permute-done.7
  47.7 1.3 collective-permute-start.8
  49.0 4.9 %collective-permute-start.9 = (f32[4,1,8,256]{3,2,1,0:T(8,128)S(1)}, f32[4,1,8,256]{3,2,1,0:T(8,128)S(1)}, u32[]{:S(2)}, u32[]{:S(2)}) collective-permute-start(f32[4,1,8,256]{3,2,1,0:T(8,128)S(1)} %get-tuple-element.28), channel_id=1, source_target_pairs={{0,16},{16,32},{32,48},{1,17},{17,33},{33,49},{2,18},{18,34},{34,5... | collective-permute-start | bytes 98312 | tf_op jit(solution)/shard_map/ppermute | solution.py:16
  53.9 1.5 collective-permute-done.9
  55.5 1.9 collective-permute-start.10
  57.4 4.6 collective-permute-start.11
  62.5 1.2 collective-permute-done.11
  63.7 1.3 fusion.15
  64.9 4.7 copy.20
  69.7 58.1 %gather_fusion.2 = f32[16384,4]{1,0:T(8,128)} fusion(f32[4,16384]{0,1:T(8,128)} %bitcast.34, s32[16384]{0:T(1024)S(1)} %broadcast_clamp_fusion), kind=kCustom, calls=%fused_computation.2 | custom fusion | bytes 589824 | tf_op jit(solution)/shard_map/gather | solution.py:99
  127.8 13.0 %bitcast_reduce_fusion = f32[2048,4]{1,0:T(8,128)S(1)} fusion(f32[16384,4]{1,0:T(8,128)} %gather_fusion.2), kind=kLoop, calls=%fused_computation.7 | loop fusion | flops 57344 | bytes 294912 | tf_op jit(solution)/shard_map/reduce_sum | solution.py:99
  142.4 65.4 %psum.21 = f32[4]{0:T(128)S(1)} all-reduce(f32[4]{0:T(128)S(1)} %multiply_reduce_fusion), channel_id=1, replica_groups=mesh['test'=8,'bx'=4,'by'=16] {'by'}, use_global_device_ids=true, to_apply=%region_3.4 | all-reduce | flops 4 | bytes 32 | tf_op jit(solution)/shard_map/psum | solution.py:103
  207.9 1.5 compare_select_fusion.1
  209.4 12.8 %psum.22 = f32[4]{0:T(128)S(1)} all-reduce(f32[4]{0:T(128)S(1)} %psum.21), channel_id=1, replica_groups=mesh['test'=8,'bx'=4,'by'=16] {'bx'}, use_global_device_ids=true, to_apply=%region_4.5 | all-reduce | flops 4 | bytes 32 | tf_op jit(solution)/shard_map/psum | solution.py:103
  222.7 91.6 %scatter_custom_fusion.1 = f32[4,16384]{0,1:T(8,128)} fusion(s32[16384]{0:T(1024)} %bitcast.41, f32[4,2048]{0,1:T(8,128)S(1)} %broadcast_divide_fusion, f32[]{:T(128)} %constant.27.clone.1), kind=kCustom, calls=%fused_computation.5 | custom fusion | flops 65536 | bytes 295424 | tf_op jit(solution)/shard_map/scatter-add | solution.py:110
  314.2 5.2 %copy.24 = f32[4,8,8,256]{3,2,1,0:T(8,128)S(1)} copy(f32[4,8,8,256]{0,3,2,1:T(8,128)} %bitcast.38) | data formatting | bytes 524288 | tf_op jit(solution)/shard_map/reshape | solution.py:113
  319.5 1.3 collective-permute-start.12
  320.8 4.5 collective-permute-start.13
  325.4 1.6 collective-permute-done.13
  327.0 3.9 collective-permute-start.14
  330.9 1.9 collective-permute-start.15
  332.9 3.9 collective-permute-done.15
  337.1 1.3 collective-permute-start.16
  338.4 4.9 %collective-permute-start.17 = (f32[4,1,8,256]{3,2,1,0:T(8,128)S(1)}, f32[4,1,8,256]{3,2,1,0:T(8,128)S(1)}, u32[]{:S(2)}, u32[]{:S(2)}) collective-permute-start(f32[4,1,8,256]{3,2,1,0:T(8,128)S(1)} %get-tuple-element.24), channel_id=1, source_target_pairs={{0,16},{16,32},{32,48},{1,17},{17,33},{33,49},{2,18},{18,34},{34,5... | collective-permute-start | bytes 98312 | tf_op jit(solution)/shard_map/ppermute | solution.py:16
  343.3 1.6 collective-permute-done.17
  344.9 1.9 collective-permute-start.18
  346.9 3.9 collective-permute-start.19
  350.8 1.9 collective-permute-done.19
  353.0 1.3 collective-permute-start.20
  354.3 4.9 %collective-permute-start.21 = (f32[8,1,8,256]{3,2,1,0:T(8,128)S(1)}, f32[8,1,8,256]{3,2,1,0:T(8,128)S(1)}, u32[]{:S(2)}, u32[]{:S(2)}) collective-permute-start(f32[8,1,8,256]{3,2,1,0:T(8,128)S(1)} %get-tuple-element.14), channel_id=1, source_target_pairs={{0,16},{16,32},{32,48},{1,17},{17,33},{33,49},{2,18},{18,34},{34,5... | collective-permute-start | bytes 196616 | tf_op jit(solution)/shard_map/ppermute | solution.py:16
  359.5 1.6 collective-permute-done.21
  361.2 1.9 collective-permute-start.22
  363.1 3.9 collective-permute-start.23
  367.5 1.9 collective-permute-done.23
  370.6 102.6 %all-reduce.9.cloned.1.call-done = f32[8,8,256]{2,1,0:T(8,128)} async-done(((f32[8,8,256]{2,1,0:T(8,128)}), f32[8,8,256]{2,1,0:T(8,128)}) %all-reduce.9.cloned.1.call-update) | async-done | bytes 65552 | tf_op jit(solution)/shard_map/psum | solution.py:150
  473.2 1.4 dynamic-slice_multiply_fusion
  (82 shorter events, 12.2 us)
Async XLA Ops:
  6.5 55.5 %copy-start = (s32[2048]{0:T(1024)S(1)}, s32[2048]{0:T(1024)}, u32[]{:S(2)}) copy-start(s32[2048]{0:T(1024)} %param.15) | copy-start | bytes 24580
  6.5 55.6 %copy-start.11 = (f32[4,2048]{1,0:T(4,128)S(1)}, f32[4,2048]{1,0:T(4,128)}, u32[]{:S(2)}) copy-start(f32[4,2048]{1,0:T(4,128)} %param.14) | copy-start | bytes 98308
  6.5 466.6 %all-reduce.9.cloned.1.call-start = ((), (), s32[]{:S(2)}) async-start(), calls=%async_computation | async-start | bytes 131072 | tf_op jit(solution)/shard_map/psum | solution.py:150
  7.3 8.4 %collective-permute-start.1 = (f32[1,8,256]{2,1,0:T(8,128)S(1)}, f32[1,8,256]{2,1,0:T(8,128)S(1)}, u32[]{:S(2)}, u32[]{:S(2)}) collective-permute-start(f32[1,8,256]{2,1,0:T(8,128)S(1)} %get-tuple-element.35), channel_id=1, source_target_pairs={{0,16},{16,32},{32,48},{1,17},{17,33},{33,49},{2,18},{18,34},{34,5... | collective-permute-start | bytes 24584 | tf_op jit(solution)/shard_map/ppermute | solution.py:16
  10.8 5.8 %collective-permute-start = (f32[1,8,256]{2,1,0:T(8,128)S(1)}, f32[1,8,256]{2,1,0:T(8,128)S(1)}, u32[]{:S(2)}, u32[]{:S(2)}) collective-permute-start(f32[1,8,256]{2,1,0:T(8,128)S(1)} %get-tuple-element.34), channel_id=1, source_target_pairs={{16,0},{32,16},{48,32},{17,1},{33,17},{49,33},{18,2},{34,18},{50,3... | collective-permute-start | bytes 24584 | tf_op jit(solution)/shard_map/ppermute | solution.py:19
  16.6 11.5 %collective-permute-start.2 = (f32[10,1,256]{2,1,0:T(1,128)S(1)}, f32[10,1,256]{2,1,0:T(1,128)S(1)}, u32[]{:S(2)}, u32[]{:S(2)}) collective-permute-start(f32[10,1,256]{2,1,0:T(1,128)S(1)} %get-tuple-element.33), channel_id=1, source_target_pairs={{1,0},{2,1},{3,2},{4,3},{5,4},{6,5},{7,6},{8,7},{9,8},{10,9},{11,1... | collective-permute-start | bytes 30728 | tf_op jit(solution)/shard_map/ppermute | solution.py:19
  22.2 5.9 %collective-permute-start.3 = (f32[10,1,256]{2,1,0:T(1,128)S(1)}, f32[10,1,256]{2,1,0:T(1,128)S(1)}, u32[]{:S(2)}, u32[]{:S(2)}) collective-permute-start(f32[10,1,256]{2,1,0:T(1,128)S(1)} %get-tuple-element.32), channel_id=1, source_target_pairs={{0,1},{1,2},{2,3},{3,4},{4,5},{5,6},{6,7},{7,8},{8,9},{9,10},{10,1... | collective-permute-start | bytes 30728 | tf_op jit(solution)/shard_map/ppermute | solution.py:16
  29.3 32.7 %copy-start.1 = (f32[8,8,256]{2,1,0:T(8,128)}, f32[8,8,256]{2,1,0:T(8,128)S(1)}, u32[]{:S(2)}) copy-start(f32[8,8,256]{2,1,0:T(8,128)S(1)} %get-tuple-element.7) | copy-start | bytes 196612
  29.4 32.7 %copy-start.3 = (f32[8,8,256]{2,1,0:T(8,128)}, f32[8,8,256]{2,1,0:T(8,128)S(1)}, u32[]{:S(2)}) copy-start(f32[8,8,256]{2,1,0:T(8,128)S(1)} %get-tuple-element.8) | copy-start | bytes 196612
  29.4 32.7 %copy-start.5 = (f32[8,8,256]{2,1,0:T(8,128)}, f32[8,8,256]{2,1,0:T(8,128)S(1)}, u32[]{:S(2)}) copy-start(f32[8,8,256]{2,1,0:T(8,128)S(1)} %get-tuple-element.9) | copy-start | bytes 196612
  29.4 32.7 %copy-start.7 = (f32[8,8,256]{2,1,0:T(8,128)}, f32[8,8,256]{2,1,0:T(8,128)S(1)}, u32[]{:S(2)}) copy-start(f32[8,8,256]{2,1,0:T(8,128)S(1)} %get-tuple-element.10) | copy-start | bytes 196612
  29.4 32.7 %copy-start.9 = (f32[8,8,256]{2,1,0:T(8,128)}, f32[8,8,256]{2,1,0:T(8,128)S(1)}, u32[]{:S(2)}) copy-start(f32[8,8,256]{2,1,0:T(8,128)S(1)} %get-tuple-element.11) | copy-start | bytes 196612
  29.5 6.5 %collective-permute-start.4 = (f32[4,1,8,256]{3,2,1,0:T(8,128)S(1)}, f32[4,1,8,256]{3,2,1,0:T(8,128)S(1)}, u32[]{:S(2)}, u32[]{:S(2)}) collective-permute-start(f32[4,1,8,256]{3,2,1,0:T(8,128)S(1)} %get-tuple-element.31), channel_id=1, source_target_pairs={{16,0},{32,16},{48,32},{17,1},{33,17},{49,33},{18,2},{34,18},{50,3... | collective-permute-start | bytes 98312 | tf_op jit(solution)/shard_map/ppermute | solution.py:19
  30.8 6.8 %collective-permute-start.5 = (f32[4,1,8,256]{3,2,1,0:T(8,128)S(1)}, f32[4,1,8,256]{3,2,1,0:T(8,128)S(1)}, u32[]{:S(2)}, u32[]{:S(2)}) collective-permute-start(f32[4,1,8,256]{3,2,1,0:T(8,128)S(1)} %get-tuple-element.30), channel_id=1, source_target_pairs={{0,16},{16,32},{32,48},{1,17},{17,33},{33,49},{2,18},{18,34},{34,5... | collective-permute-start | bytes 98312 | tf_op jit(solution)/shard_map/ppermute | solution.py:16
  37.6 6.7 %collective-permute-start.6 = (f32[4,10,1,256]{3,2,1,0:T(1,128)S(1)}, f32[4,10,1,256]{3,2,1,0:T(1,128)S(1)}, u32[]{:S(2)}, u32[]{:S(2)}) collective-permute-start(f32[4,10,1,256]{3,2,1,0:T(1,128)S(1)} %get-tuple-element.22), channel_id=1, source_target_pairs={{1,0},{2,1},{3,2},{4,3},{5,4},{6,5},{7,6},{8,7},{9,8},{10,9},{11,1... | collective-permute-start | bytes 122888 | tf_op jit(solution)/shard_map/ppermute | solution.py:19
  41.5 5.9 %collective-permute-start.7 = (f32[4,10,1,256]{3,2,1,0:T(1,128)S(1)}, f32[4,10,1,256]{3,2,1,0:T(1,128)S(1)}, u32[]{:S(2)}, u32[]{:S(2)}) collective-permute-start(f32[4,10,1,256]{3,2,1,0:T(1,128)S(1)} %get-tuple-element.23), channel_id=1, source_target_pairs={{0,1},{1,2},{2,3},{3,4},{4,5},{5,6},{6,7},{7,8},{8,9},{9,10},{10,1... | collective-permute-start | bytes 122888 | tf_op jit(solution)/shard_map/ppermute | solution.py:16
  47.7 6.2 %collective-permute-start.8 = (f32[4,1,8,256]{3,2,1,0:T(8,128)S(1)}, f32[4,1,8,256]{3,2,1,0:T(8,128)S(1)}, u32[]{:S(2)}, u32[]{:S(2)}) collective-permute-start(f32[4,1,8,256]{3,2,1,0:T(8,128)S(1)} %get-tuple-element.29), channel_id=1, source_target_pairs={{16,0},{32,16},{48,32},{17,1},{33,17},{49,33},{18,2},{34,18},{50,3... | collective-permute-start | bytes 98312 | tf_op jit(solution)/shard_map/ppermute | solution.py:19
  49.0 6.4 %collective-permute-start.9 = (f32[4,1,8,256]{3,2,1,0:T(8,128)S(1)}, f32[4,1,8,256]{3,2,1,0:T(8,128)S(1)}, u32[]{:S(2)}, u32[]{:S(2)}) collective-permute-start(f32[4,1,8,256]{3,2,1,0:T(8,128)S(1)} %get-tuple-element.28), channel_id=1, source_target_pairs={{0,16},{16,32},{32,48},{1,17},{17,33},{33,49},{2,18},{18,34},{34,5... | collective-permute-start | bytes 98312 | tf_op jit(solution)/shard_map/ppermute | solution.py:16
  55.5 7.0 %collective-permute-start.10 = (f32[4,10,1,256]{3,2,1,0:T(1,128)S(1)}, f32[4,10,1,256]{3,2,1,0:T(1,128)S(1)}, u32[]{:S(2)}, u32[]{:S(2)}) collective-permute-start(f32[4,10,1,256]{3,2,1,0:T(1,128)S(1)} %get-tuple-element.20), channel_id=1, source_target_pairs={{1,0},{2,1},{3,2},{4,3},{5,4},{6,5},{7,6},{8,7},{9,8},{10,9},{11,1... | collective-permute-start | bytes 122888 | tf_op jit(solution)/shard_map/ppermute | solution.py:19
  57.4 6.2 %collective-permute-start.11 = (f32[4,10,1,256]{3,2,1,0:T(1,128)S(1)}, f32[4,10,1,256]{3,2,1,0:T(1,128)S(1)}, u32[]{:S(2)}, u32[]{:S(2)}) collective-permute-start(f32[4,10,1,256]{3,2,1,0:T(1,128)S(1)} %get-tuple-element.21), channel_id=1, source_target_pairs={{0,1},{1,2},{2,3},{3,4},{4,5},{5,6},{6,7},{7,8},{8,9},{9,10},{10,1... | collective-permute-start | bytes 122888 | tf_op jit(solution)/shard_map/ppermute | solution.py:16
  222.6 114.2 %copy-start.2 = (f32[8,8,256]{2,1,0:T(8,128)S(1)}, f32[8,8,256]{2,1,0:T(8,128)}, u32[]{:S(2)}) copy-start(f32[8,8,256]{2,1,0:T(8,128)} %copy-done.1) | copy-start | bytes 196612
  222.6 114.2 %copy-start.4 = (f32[8,8,256]{2,1,0:T(8,128)S(1)}, f32[8,8,256]{2,1,0:T(8,128)}, u32[]{:S(2)}) copy-start(f32[8,8,256]{2,1,0:T(8,128)} %copy-done.3) | copy-start | bytes 196612
  222.6 114.2 %copy-start.6 = (f32[8,8,256]{2,1,0:T(8,128)S(1)}, f32[8,8,256]{2,1,0:T(8,128)}, u32[]{:S(2)}) copy-start(f32[8,8,256]{2,1,0:T(8,128)} %copy-done.5) | copy-start | bytes 196612
  222.6 114.2 %copy-start.8 = (f32[8,8,256]{2,1,0:T(8,128)S(1)}, f32[8,8,256]{2,1,0:T(8,128)}, u32[]{:S(2)}) copy-start(f32[8,8,256]{2,1,0:T(8,128)} %copy-done.7) | copy-start | bytes 196612
  222.7 114.2 %copy-start.10 = (f32[8,8,256]{2,1,0:T(8,128)S(1)}, f32[8,8,256]{2,1,0:T(8,128)}, u32[]{:S(2)}) copy-start(f32[8,8,256]{2,1,0:T(8,128)} %copy-done.9) | copy-start | bytes 196612
  319.5 5.9 %collective-permute-start.12 = (f32[4,1,8,256]{3,2,1,0:T(8,128)S(1)}, f32[4,1,8,256]{3,2,1,0:T(8,128)S(1)}, u32[]{:S(2)}, u32[]{:S(2)}) collective-permute-start(f32[4,1,8,256]{3,2,1,0:T(8,128)S(1)} %get-tuple-element.27), channel_id=1, source_target_pairs={{16,0},{32,16},{48,32},{17,1},{33,17},{49,33},{18,2},{34,18},{50,3... | collective-permute-start | bytes 98312 | tf_op jit(solution)/shard_map/ppermute | solution.py:19
  320.8 6.1 %collective-permute-start.13 = (f32[4,1,8,256]{3,2,1,0:T(8,128)S(1)}, f32[4,1,8,256]{3,2,1,0:T(8,128)S(1)}, u32[]{:S(2)}, u32[]{:S(2)}) collective-permute-start(f32[4,1,8,256]{3,2,1,0:T(8,128)S(1)} %get-tuple-element.26), channel_id=1, source_target_pairs={{0,16},{16,32},{32,48},{1,17},{17,33},{33,49},{2,18},{18,34},{34,5... | collective-permute-start | bytes 98312 | tf_op jit(solution)/shard_map/ppermute | solution.py:16
  327.0 5.9 %collective-permute-start.14 = (f32[4,10,1,256]{3,2,1,0:T(1,128)S(1)}, f32[4,10,1,256]{3,2,1,0:T(1,128)S(1)}, u32[]{:S(2)}, u32[]{:S(2)}) collective-permute-start(f32[4,10,1,256]{3,2,1,0:T(1,128)S(1)} %get-tuple-element.18), channel_id=1, source_target_pairs={{1,0},{2,1},{3,2},{4,3},{5,4},{6,5},{7,6},{8,7},{9,8},{10,9},{11,1... | collective-permute-start | bytes 122888 | tf_op jit(solution)/shard_map/ppermute | solution.py:19
  330.9 5.9 %collective-permute-start.15 = (f32[4,10,1,256]{3,2,1,0:T(1,128)S(1)}, f32[4,10,1,256]{3,2,1,0:T(1,128)S(1)}, u32[]{:S(2)}, u32[]{:S(2)}) collective-permute-start(f32[4,10,1,256]{3,2,1,0:T(1,128)S(1)} %get-tuple-element.19), channel_id=1, source_target_pairs={{0,1},{1,2},{2,3},{3,4},{4,5},{5,6},{6,7},{7,8},{8,9},{9,10},{10,1... | collective-permute-start | bytes 122888 | tf_op jit(solution)/shard_map/ppermute | solution.py:16
  337.1 6.2 %collective-permute-start.16 = (f32[4,1,8,256]{3,2,1,0:T(8,128)S(1)}, f32[4,1,8,256]{3,2,1,0:T(8,128)S(1)}, u32[]{:S(2)}, u32[]{:S(2)}) collective-permute-start(f32[4,1,8,256]{3,2,1,0:T(8,128)S(1)} %get-tuple-element.25), channel_id=1, source_target_pairs={{16,0},{32,16},{48,32},{17,1},{33,17},{49,33},{18,2},{34,18},{50,3... | collective-permute-start | bytes 98312 | tf_op jit(solution)/shard_map/ppermute | solution.py:19
  338.4 6.4 %collective-permute-start.17 = (f32[4,1,8,256]{3,2,1,0:T(8,128)S(1)}, f32[4,1,8,256]{3,2,1,0:T(8,128)S(1)}, u32[]{:S(2)}, u32[]{:S(2)}) collective-permute-start(f32[4,1,8,256]{3,2,1,0:T(8,128)S(1)} %get-tuple-element.24), channel_id=1, source_target_pairs={{0,16},{16,32},{32,48},{1,17},{17,33},{33,49},{2,18},{18,34},{34,5... | collective-permute-start | bytes 98312 | tf_op jit(solution)/shard_map/ppermute | solution.py:16
  344.9 5.9 %collective-permute-start.18 = (f32[4,10,1,256]{3,2,1,0:T(1,128)S(1)}, f32[4,10,1,256]{3,2,1,0:T(1,128)S(1)}, u32[]{:S(2)}, u32[]{:S(2)}) collective-permute-start(f32[4,10,1,256]{3,2,1,0:T(1,128)S(1)} %get-tuple-element.16), channel_id=1, source_target_pairs={{1,0},{2,1},{3,2},{4,3},{5,4},{6,5},{7,6},{8,7},{9,8},{10,9},{11,1... | collective-permute-start | bytes 122888 | tf_op jit(solution)/shard_map/ppermute | solution.py:19
  346.9 5.9 %collective-permute-start.19 = (f32[4,10,1,256]{3,2,1,0:T(1,128)S(1)}, f32[4,10,1,256]{3,2,1,0:T(1,128)S(1)}, u32[]{:S(2)}, u32[]{:S(2)}) collective-permute-start(f32[4,10,1,256]{3,2,1,0:T(1,128)S(1)} %get-tuple-element.17), channel_id=1, source_target_pairs={{0,1},{1,2},{2,3},{3,4},{4,5},{5,6},{6,7},{7,8},{8,9},{9,10},{10,1... | collective-permute-start | bytes 122888 | tf_op jit(solution)/shard_map/ppermute | solution.py:16
  353.0 6.5 %collective-permute-start.20 = (f32[8,1,8,256]{3,2,1,0:T(8,128)S(1)}, f32[8,1,8,256]{3,2,1,0:T(8,128)S(1)}, u32[]{:S(2)}, u32[]{:S(2)}) collective-permute-start(f32[8,1,8,256]{3,2,1,0:T(8,128)S(1)} %get-tuple-element.15), channel_id=1, source_target_pairs={{16,0},{32,16},{48,32},{17,1},{33,17},{49,33},{18,2},{34,18},{50,3... | collective-permute-start | bytes 196616 | tf_op jit(solution)/shard_map/ppermute | solution.py:19
  354.3 6.7 %collective-permute-start.21 = (f32[8,1,8,256]{3,2,1,0:T(8,128)S(1)}, f32[8,1,8,256]{3,2,1,0:T(8,128)S(1)}, u32[]{:S(2)}, u32[]{:S(2)}) collective-permute-start(f32[8,1,8,256]{3,2,1,0:T(8,128)S(1)} %get-tuple-element.14), channel_id=1, source_target_pairs={{0,16},{16,32},{32,48},{1,17},{17,33},{33,49},{2,18},{18,34},{34,5... | collective-permute-start | bytes 196616 | tf_op jit(solution)/shard_map/ppermute | solution.py:16
  361.2 6.3 %collective-permute-start.22 = (f32[8,10,1,256]{3,2,1,0:T(1,128)S(1)}, f32[8,10,1,256]{3,2,1,0:T(1,128)S(1)}, u32[]{:S(2)}, u32[]{:S(2)}) collective-permute-start(f32[8,10,1,256]{3,2,1,0:T(1,128)S(1)} %get-tuple-element.12), channel_id=1, source_target_pairs={{1,0},{2,1},{3,2},{4,3},{5,4},{6,5},{7,6},{8,7},{9,8},{10,9},{11,1... | collective-permute-start | bytes 245768 | tf_op jit(solution)/shard_map/ppermute | solution.py:19
  363.1 6.3 %collective-permute-start.23 = (f32[8,10,1,256]{3,2,1,0:T(1,128)S(1)}, f32[8,10,1,256]{3,2,1,0:T(1,128)S(1)}, u32[]{:S(2)}, u32[]{:S(2)}) collective-permute-start(f32[8,10,1,256]{3,2,1,0:T(1,128)S(1)} %get-tuple-element.13), channel_id=1, source_target_pairs={{0,1},{1,2},{2,3},{3,4},{4,5},{5,6},{6,7},{7,8},{8,9},{9,10},{10,1... | collective-permute-start | bytes 245768 | tf_op jit(solution)/shard_map/ppermute | solution.py:16
Sparse Core Ops, SparseCore 0:
  370.7 102.4 all-reduce.8
